TPU v7x, 32 devices: a whole 2x2x4 slice. The times are simulated.
32 devices in a mesh: particle: 2 (over x), coil: 8 (over z, y), phase: 2 (over core).
Axes of the slice: x: 2, y: 2, z: 4, core: 2. Of those that a mesh axis runs over, the one named last changes fastest.
Arguments:
- position: float32 [256, 16, 4, 384], P('coil', 'phase', 'particle'), parts along dimension 2, may hold values from -6 to 6
- coil_maps: bfloat16 [8, 256, 4, 384], P('coil', None, 'particle'), parts along dimension 2, may hold values from -2 to 2
- kspace_data: bfloat16 [8, 256, 16, 4, 384], P('coil', None, 'phase', 'particle'), parts along dimension 3, may hold values from -1.796875 to 1.796875
- sample_mask: int32 [256, 16], P(None, 'phase'), may hold values 0 or 1
Outputs:
- gradient: float32 [256, 16, 4, 384], P('coil', 'phase', 'particle'), parts along dimension 2
There are 2 independent parts, one for each index of `particle`. A program takes and returns all parts, laid end to end along the dimension named above; an argument that names none is the same for every part. Nothing has to cross between parts.
All inputs are finite; a program needn't handle non-finite values. No bound on the sum of `sample_mask` on one device may be relied on, other than what follows from the above.
Results may differ from a plain program's by a relative error of at most 0.0012.
Values may be sent and summed in bfloat16 or wider, within the bound.
A program may use at most 64 MiB of HBM per device.

v0:
```python
import math
import jax
import jax.numpy as jnp
from jax import lax
from jax.sharding import PartitionSpec as P


def with_halo(block, sides, width):
    for axis, dim in sides:
        count = lax.axis_size(axis)
        forward = [(i, i + 1) for i in range(count - 1)]
        forward.append((count - 1, 0))
        backward = [(target, source) for source, target in forward]
        low = lax.ppermute(
            lax.slice_in_dim(block, block.shape[dim] - width, None, axis=dim), axis, forward
        )
        high = lax.ppermute(lax.slice_in_dim(block, 0, width, axis=dim), axis, backward)
        block = jnp.concatenate([low, block, high], axis=dim)
    return block


def dft_tables(length):
    counter = jnp.arange(length, dtype=jnp.int32)
    product = counter[:, None] * counter[None, :] % length
    angles = product.astype(jnp.float32) * (2.0 * math.pi / length)
    scaling = 1.0 / math.sqrt(length)
    return (jnp.cos(angles) * scaling, -jnp.sin(angles) * scaling)


def build_tables(rows_total, width):
    row_real, row_imag = dft_tables(rows_total)
    col_real, col_imag = dft_tables(width)
    forward_wide = jnp.concatenate(
        [jnp.concatenate([col_real, col_imag], 1), jnp.concatenate([-col_imag, col_real], 1)], 0
    )
    backward_wide = jnp.concatenate(
        [jnp.concatenate([col_real, -col_imag], 1), jnp.concatenate([col_imag, col_real], 1)], 0
    )
    return (
        row_real.astype(jnp.bfloat16),
        row_imag.astype(jnp.bfloat16),
        forward_wide.astype(jnp.bfloat16),
        backward_wide.astype(jnp.bfloat16),
    )


def complex_times(factor, values, conjugate):
    width = values.shape[-1] // 2
    factor_real = factor[..., :width]
    factor_imag = factor[..., width:]
    if conjugate:
        factor_imag = -factor_imag
    value_real = values[..., :width]
    value_imag = values[..., width:]
    out_real = factor_real * value_real - factor_imag * value_imag
    out_imag = factor_real * value_imag + factor_imag * value_real
    return jnp.concatenate([out_real, out_imag], -1)


def rows_apply(table_real, table_imag, values, adjoint):
    width = values.shape[-1] // 2
    real_part = jnp.einsum("kn,npsd->kpsd", table_real, values, preferred_element_type=jnp.float32)
    imag_part = jnp.einsum("kn,npsd->kpsd", table_imag, values, preferred_element_type=jnp.float32)
    if adjoint:
        out_real = real_part[..., :width] + imag_part[..., width:]
        out_imag = real_part[..., width:] - imag_part[..., :width]
    else:
        out_real = real_part[..., :width] - imag_part[..., width:]
        out_imag = real_part[..., width:] + imag_part[..., :width]
    return jnp.concatenate([out_real, out_imag], -1)


def local(position, coil_maps, kspace_data, sample_mask):
    rows_here = position.shape[0]
    rows_total = coil_maps.shape[1]
    width = position.shape[3] // 2
    row_real, row_imag, forward_wide, backward_wide = build_tables(rows_total, width)
    coil_map = coil_maps[0]
    coil_data = kspace_data[0]
    sample_weight = sample_mask.astype(jnp.float32)[:, :, None, None]
    position_low = position.astype(jnp.bfloat16)
    map_rows = coil_map.astype(jnp.float32)[:, None]
    lifted = complex_times(
        map_rows,
        lax.all_gather(position_low, "coil", axis=0, tiled=True).astype(jnp.float32),
        False,
    ).astype(jnp.bfloat16)
    spread = jnp.einsum(
        "npsc,cd->npsd", lifted, forward_wide, preferred_element_type=jnp.float32
    ).astype(jnp.bfloat16)
    kspace = rows_apply(row_real, row_imag, spread, False)
    residual = (sample_weight * (kspace - coil_data.astype(jnp.float32))).astype(jnp.bfloat16)
    back_rows = rows_apply(row_real, row_imag, residual, True).astype(jnp.bfloat16)
    back = jnp.einsum("npsc,cd->npsd", back_rows, backward_wide, preferred_element_type=jnp.float32)
    map_rows = coil_map.astype(jnp.float32)[:, None]
    summed = lax.psum(complex_times(map_rows, back, True), "coil")
    likelihood = lax.dynamic_slice_in_dim(summed, lax.axis_index("coil") * rows_here, rows_here, 0)
    padded = with_halo(position, (("coil", 0), ("phase", 1)), 1)
    phase_part = 2.0 * position - padded[1:-1, :-2] - padded[1:-1, 2:]
    row_part = 2.0 * position - padded[:-2, 1:-1] - padded[2:, 1:-1]
    return 0.6 * likelihood + 0.5 * phase_part + 0.3 * row_part


def solution(mesh):
    in_specs = (
        P("coil", "phase", "particle", None),
        P("coil", None, "particle", None),
        P("coil", None, "phase", "particle", None),
        P(None, "phase"),
    )
    out_specs = P("coil", "phase", "particle", None)
    return jax.shard_map(local, mesh=mesh, in_specs=in_specs, out_specs=out_specs, check_vma=False)
```

profile of v0, /device:TPU:0, one launch (start us, length us, event | category | flops | bytes accessed | tf_op | source)
XLA Modules:
  0.0 333.7 jit_solution(8550984614529454720)
XLA Ops:
  6.5 2.1 copy.23
  8.8 1.3 bitcast_convert_fusion
  10.9 0.9 copy.9
  12.6 0.8 negate_convert_fusion
  13.4 58.9 %all-gather.2.cloned.1.call-done = bf16[256,8,2,384]{3,0,2,1:T(8,128)(2,1)} async-done(((bf16[32,8,2,384]{3,0,2,1:T(8,128)(2,1)}), bf16[256,8,2,384]{3,0,2,1:T(8,128)(2,1)}) %all-gather.2.cloned.1.call-update) | async-done | bytes 3145744 | tf_op jit(solution)/shard_map/all_gather | solution.py:85
  72.3 2.5 convert_element_type.81
  74.9 1.8 subtract_convert_fusion
  76.7 2.3 fusion.12
  79.0 1.9 fusion.49
  80.9 4.6 %fusion.53 = f32[256,8,2,384]{3,0,2,1:T(8,128)} fusion(bf16[256,8,2,384]{3,0,2,1:T(8,128)(2,1)S(1)} %fusion.12), kind=kOutput, calls=%fused_computation.82 | convolution fusion | flops 806354944 | bytes 9437184 | tf_op jit(solution)/shard_map/kn,npsd->kpsd/dot_general | solution.py:62
  85.4 9.2 %slice_subtract_fusion.1 = (f32[256,8,2,192]{3,0,2,1:T(8,128)}, f32[256,8,2,192]{3,0,2,1:T(8,128)}) fusion(f32[256,8,2,384]{3,0,2,1:T(8,128)S(1)} %fusion.49, f32[256,8,2,384]{3,0,2,1:T(8,128)} %fusion.53), kind=kLoop, calls=%fused_computation.9 | loop fusion | flops 1572864 | bytes 18874368 | tf_op jit(solution)/shard_map/sub | solution.py:68
  94.7 5.3 %fusion.1 = bf16[256,8,2,384]{3,0,2,1:T(8,128)(2,1)S(1)} fusion(f32[256,8,2,192]{3,0,2,1:T(8,128)} %get-tuple-element.8, f32[256,8,2,192]{3,0,2,1:T(8,128)} %get-tuple-element.7, bf16[1,256,8,2,384]{4,3,2,1,0:T(2,128)(2,1)} %param.6, f32[256,8]{0,1:T(8,128)S(1)} %convert_element_type.79), kind=kLoop, calls=%fused_computation.2 | loop fusion | flops 7864320 | bytes 12591104 | tf_op jit(solution)/shard_map/convert_element_type | solution.py:92
  100.0 1.9 fusion.47
  101.9 1.9 fusion.51
  103.8 2.6 fusion.3
  106.4 2.3 fusion.8
  108.7 2.0 multiply_subtract_fusion
  110.8 3.9 %pad_maximum_fusion = f32[256,8,2,384]{3,0,2,1:T(8,128)} fusion(f32[256,8,2,192]{3,0,2,1:T(8,128)S(1)} %get-tuple-element.10, f32[256,8,2,192]{3,0,2,1:T(8,128)S(1)} %get-tuple-element.9), kind=kLoop, calls=%fused_computation.3 | loop fusion | flops 1572864 | bytes 12582912 | tf_op jit(solution)/shard_map/concatenate | solution.py:57
  114.7 1.1 copy-done.2
  116.5 4.2 %collective-permute-start.1 = (f32[1,8,2,384]{3,0,2,1:T(1,128)S(1)}, f32[1,8,2,384]{3,0,2,1:T(1,128)S(1)}, u32[]{:S(2)}, u32[]{:S(2)}) collective-permute-start(f32[1,8,2,384]{3,0,2,1:T(1,128)S(1)} %copy.12), channel_id=1, source_target_pairs={{2,0},{4,2},{6,4},{8,6},{10,8},{12,10},{14,12},{0,14},{3,1},{5,3},... | collective-permute-start | bytes 73736 | tf_op jit(solution)/shard_map/ppermute | solution.py:17
  121.0 1.6 collective-permute-done
  124.3 199.5 %all-reduce.2.cloned.1.call-done = f32[256,8,2,384]{3,0,2,1:T(8,128)} async-done(((f32[256,8,2,384]{3,0,2,1:T(8,128)}), f32[256,8,2,384]{3,0,2,1:T(8,128)}) %all-reduce.2.cloned.1.call-update) | async-done | bytes 6291472 | tf_op jit(solution)/shard_map/psum | solution.py:96
  323.8 1.6 fusion.17
  325.4 1.5 copy.16
  (29 shorter events, 4.4 us)
Async XLA Ops:
  6.5 4.3 %copy-start.4 = (s32[256,8]{0,1:T(8,128)S(1)}, s32[256,8]{0,1:T(8,128)}, u32[]{:S(2)}) copy-start(s32[256,8]{0,1:T(8,128)} %param.7) | copy-start | bytes 24580
  6.5 65.8 %all-gather.2.cloned.1.call-start = ((), (), s32[]{:S(2)}) async-start(), calls=%async_computation | async-start | bytes 3538944 | tf_op jit(solution)/shard_map/all_gather | solution.py:85
  8.7 315.1 %all-reduce.2.cloned.1.call-start = ((), (), s32[]{:S(2)}) async-start(), calls=%async_computation.1 | async-start | bytes 12582912 | tf_op jit(solution)/shard_map/psum | solution.py:96
  10.8 64.0 %copy-start = (f32[256,2,192]{2,0,1:T(8,128)}, f32[256,2,192]{2,0,1:T(8,128)S(1)}, u32[]{:S(2)}) copy-start(f32[256,2,192]{2,0,1:T(8,128)S(1)} %copy.5) | copy-start | bytes 1179652
  106.4 2.3 copy-start.1
  106.4 2.3 copy-start.3
  114.7 1.1 copy-start.2
  115.9 6.7 %collective-permute-start = (f32[1,8,2,384]{3,0,2,1:T(1,128)S(1)}, f32[1,8,2,384]{3,0,2,1:T(1,128)S(1)}, u32[]{:S(2)}, u32[]{:S(2)}) collective-permute-start(f32[1,8,2,384]{3,0,2,1:T(1,128)S(1)} %copy.11), channel_id=1, source_target_pairs={{0,2},{2,4},{4,6},{6,8},{8,10},{10,12},{12,14},{14,0},{1,3},{3,5},... | collective-permute-start | bytes 73736 | tf_op jit(solution)/shard_map/ppermute | solution.py:14
  116.5 6.2 %collective-permute-start.1 = (f32[1,8,2,384]{3,0,2,1:T(1,128)S(1)}, f32[1,8,2,384]{3,0,2,1:T(1,128)S(1)}, u32[]{:S(2)}, u32[]{:S(2)}) collective-permute-start(f32[1,8,2,384]{3,0,2,1:T(1,128)S(1)} %copy.12), channel_id=1, source_target_pairs={{2,0},{4,2},{6,4},{8,6},{10,8},{12,10},{14,12},{0,14},{3,1},{5,3},... | collective-permute-start | bytes 73736 | tf_op jit(solution)/shard_map/ppermute | solution.py:17
  122.8 1.4 collective-permute-start.2
  122.8 1.5 collective-permute-start.3
Sparse Core Ops, SparseCore 0:
  9.5 62.7 all-gather.1
  114.8 208.9 all-reduce.1
where the time goes:
time: 334 us
  waiting for transfers between devices  261 us (78%)
  other arithmetic  32.7 us (10%)
  matrix products  14.8 us (4%)
  between operations  13.6 us (4%)
  local copies, waits for them, and re-layouts  6.04 us (2%)
  starting transfers between devices  5.44 us (2%)
    psum x1, waiting for transfers between devices, local(): summed = lax.psum(complex_times(map_rows, back, True), 'coil')  199 us
    all_gather x1, waiting for transfers between devices, local(): lax.all_gather(position_low, 'coil', axis=0, tiled=True).astype(jnp.float32)  58.9 us
    sub x1, other arithmetic, rows_apply(): out_real = real_part[..., :width] - imag_part[..., width:]  9.23 us
  transfers between devices with their start and end apart: 6, of which 6 were waited for; matrix products, arithmetic and copies ran while one was open for 1% of the time, Pallas kernels for 0%

commit v1 on v0

--- a/solution.py
+++ b/solution.py
@@ -3,6 +3,7 @@
 import jax.numpy as jnp
 from jax import lax
 from jax.sharding import PartitionSpec as P
+from jax.lax import all_gather
 
 
 def with_halo(block, sides, width):
@@ -93,7 +94,12 @@
     back_rows = rows_apply(row_real, row_imag, residual, True).astype(jnp.bfloat16)
     back = jnp.einsum("npsc,cd->npsd", back_rows, backward_wide, preferred_element_type=jnp.float32)
     map_rows = coil_map.astype(jnp.float32)[:, None]
-    summed = lax.psum(complex_times(map_rows, back, True), "coil")
+
+    def find_the_cubes(mine_x, chip_axis):
+        r1 = all_gather(mine_x, chip_axis).sum(axis=0)
+        return r1
+
+    summed = find_the_cubes(complex_times(map_rows, back, True), "coil")
     likelihood = lax.dynamic_slice_in_dim(summed, lax.axis_index("coil") * rows_here, rows_here, 0)
     padded = with_halo(position, (("coil", 0), ("phase", 1)), 1)
     phase_part = 2.0 * position - padded[1:-1, :-2] - padded[1:-1, 2:]

time: 334 us -> 1100 us (3.29)
  waiting for transfers between devices: 261 us -> 1000 us
  other arithmetic: 32.7 us -> 52.9 us
    all_gather x0 -> x1, waiting for transfers between devices: none -> 943 us  [find_the_cubes(): r1 = all_gather(mine_x, chip_axis).sum(axis=0)]
    psum x1 -> x0, waiting for transfers between devices: 199 us -> none  [local(): summed = lax.psum(complex_times(map_rows, back, True), 'coil')]
    reduce_sum x0 -> x1, other arithmetic: none -> 20.2 us  [find_the_cubes(): r1 = all_gather(mine_x, chip_axis).sum(axis=0)]
  transfers between devices with their start and end apart: 6 -> 6, of which waited for: 6 -> 4; matrix products, arithmetic and copies ran while one was open for 1% -> 2% of each run, Pallas kernels for 0% -> 0%
where the time goes in v1:
time: 1100 us
  waiting for transfers between devices  1000 us (91%)
  other arithmetic  52.9 us (5%)
  matrix products  14.8 us (1%)
  between operations  13.6 us (1%)
    all_gather x1, waiting for transfers between devices, find_the_cubes(): r1 = all_gather(mine_x, chip_axis).sum(axis=0)  943 us
    all_gather x1, waiting for transfers between devices, local(): lax.all_gather(position_low, 'coil', axis=0, tiled=True).astype(jnp.float32)  58.9 us
  transfers between devices with their start and end apart: 6, of which 4 were waited for; matrix products, arithmetic and copies ran while one was open for 2% of the time, Pallas kernels for 0%

profile of v1, /device:TPU:0, one launch (start us, length us, event | category | flops | bytes accessed | tf_op | source)
XLA Modules:
  0.0 1096.2 jit_solution(2269197996824591500)
XLA Ops:
  6.5 2.1 copy.28
  8.8 1.3 bitcast_convert_fusion
  10.9 0.9 copy.14
  13.4 58.9 %all-gather.4.cloned.1.call-done = bf16[256,8,2,384]{3,0,2,1:T(8,128)(2,1)} async-done(((bf16[32,8,2,384]{3,0,2,1:T(8,128)(2,1)}), bf16[256,8,2,384]{3,0,2,1:T(8,128)(2,1)}) %all-gather.4.cloned.1.call-update) | async-done | bytes 3145744 | tf_op jit(solution)/shard_map/all_gather | solution.py:86
  72.3 2.5 convert_element_type.81
  74.9 1.8 subtract_convert_fusion
  76.7 2.3 fusion.12
  79.0 1.9 fusion.49
  80.9 4.6 fusion.53
  85.4 9.2 slice_subtract_fusion.1
  94.7 5.3 fusion.1
  100.0 1.9 fusion.47
  101.9 1.9 fusion.51
  103.8 2.6 fusion.3
  106.4 2.3 fusion.8
  108.7 2.0 multiply_subtract_fusion
  110.8 3.9 pad_maximum_fusion
  114.7 1.1 copy-done.2
  116.5 4.2 collective-permute-start.1
  121.0 1.6 collective-permute-done
  123.3 942.7 %all-gather.6.cloned.1.call-done = f32[2048,8,2,384]{3,0,2,1:T(8,128)} async-done(((f32[256,8,2,384]{3,0,2,1:T(8,128)}), f32[2048,8,2,384]{3,0,2,1:T(8,128)}) %all-gather.6.cloned.1.call-update) | async-done | bytes 50331664 | tf_op jit(solution)/shard_map/all_gather | solution.py:99
  1066.0 20.2 %reduce_sum.9 = f32[256,8,2,384]{3,0,2,1:T(8,128)} reduce(f32[8,256,8,2,384]{4,1,0,3,2:T(8,128)} %bitcast.39, f32[]{:T(128)} %constant.45.clone.1), dimensions={0}, to_apply=%region_0.1 | reduce | flops 11010048 | bytes 56623108 | tf_op jit(solution)/shard_map/reduce_sum | solution.py:99
  1086.3 1.6 fusion.17
  1087.9 1.5 copy.21
  (30 shorter events, 4.2 us)
Async XLA Ops:
  6.5 4.3 copy-start.4
  6.5 65.8 %all-gather.4.cloned.1.call-start = ((), (), s32[]{:S(2)}) async-start(), calls=%async_computation | async-start | bytes 3538944 | tf_op jit(solution)/shard_map/all_gather | solution.py:86
  8.7 1057.3 %all-gather.6.cloned.1.call-start = ((), (), s32[]{:S(2)}) async-start(), calls=%async_computation.1 | async-start | bytes 56623104 | tf_op jit(solution)/shard_map/all_gather | solution.py:99
  10.8 64.0 %copy-start = (f32[256,2,192]{2,0,1:T(8,128)}, f32[256,2,192]{2,0,1:T(8,128)S(1)}, u32[]{:S(2)}) copy-start(f32[256,2,192]{2,0,1:T(8,128)S(1)} %copy.10) | copy-start | bytes 1179652
  106.4 2.3 copy-start.1
  106.4 2.3 copy-start.3
  114.7 1.1 copy-start.2
  115.9 6.7 collective-permute-start
  116.5 6.2 collective-permute-start.1
  122.7 963.5 %collective-permute-start.2 = (f32[34,1,2,384]{3,0,2,1:T(8,128)S(1)}, f32[34,1,2,384]{3,0,2,1:T(8,128)S(1)}, u32[]{:S(2)}, u32[]{:S(2)}) collective-permute-start(f32[34,1,2,384]{3,0,2,1:T(8,128)S(1)} %get-tuple-element.13), channel_id=1, source_target_pairs={{0,1},{1,0},{2,3},{3,2},{4,5},{5,4},{6,7},{7,6},{8,9},{9,8},{10,11... | collective-permute-start | bytes 313352 | tf_op jit(solution)/shard_map/ppermute | solution.py:15
  122.8 963.5 %collective-permute-start.3 = (f32[34,1,2,384]{3,0,2,1:T(8,128)S(1)}, f32[34,1,2,384]{3,0,2,1:T(8,128)S(1)}, u32[]{:S(2)}, u32[]{:S(2)}) collective-permute-start(f32[34,1,2,384]{3,0,2,1:T(8,128)S(1)} %get-tuple-element.14), channel_id=1, source_target_pairs={{1,0},{0,1},{3,2},{2,3},{5,4},{4,5},{7,6},{6,7},{9,8},{8,9},{11,10... | collective-permute-start | bytes 313352 | tf_op jit(solution)/shard_map/ppermute | solution.py:18
Sparse Core Ops, SparseCore 0:
  9.5 62.7 all-gather.3
  114.8 951.1 all-gather.5
